TPU v7x, 32 devices: a whole 2x2x4 slice. The times are simulated.
32 devices in a mesh: obs: 16 (over z, x, core), cell: 2 (over y).
Axes of the slice: x: 2, y: 2, z: 4, core: 2. Of those that a mesh axis runs over, the one named last changes fastest.
Arguments:
- flux_field: bfloat16 [2, 16, 64, 128], P('cell', 'obs'), may hold values from -6 to 6
- footprint: bfloat16 [256, 16, 128, 128], P('obs', 'cell'), may hold values from -0.125 to 0.125
- block_index: int32 [256, 16], P('obs', 'cell'), may hold values from 0 to 15
- tile_count: int32 [16], P('obs'), may hold values from 1 to 16, 128 in all
- sounding_week: int32 [256, 128], P('obs'), may hold values from 0 to 3
- member_ids: int32 [16], replicated, may hold values from 0 to 15, each once
- observed: float32 [256, 128], P('obs'), may hold values from -6 to 6
- perturb: bfloat16 [256, 16, 128], P('obs'), may hold values from -6 to 6
- obs_weight: float32 [256, 128], P('obs'), may hold values from 0.3 to 3
Outputs:
- gradient: float32 [2, 16, 64, 128], P('cell', 'obs')
- residual: bfloat16 [256, 16, 128], P('obs')
All inputs are finite; a program needn't handle non-finite values. No bound on the sum of `tile_count` on one device may be relied on, other than what follows from the above.
Results may differ from a plain program's by a relative error of at most 0.0028.
Values may be sent and summed in bfloat16 or wider, within the bound.
No kernel may reach another device: no remote copies, remote signals or barrier semaphores. Data moves between devices by JAX's collectives and lax.ppermute only.
A program may use at most 64 MiB of HBM per device.

v0:
```python
import jax
import jax.numpy as jnp
from jax import lax
from jax.sharding import PartitionSpec as P

MEMBERS = 16
WEEKS = 4


def weigh_misfit(modeled, alive, weights, seen, shifted):
    return (
        alive[:, None, None] * weights[:, None, :] * (modeled - seen[:, None, :] - shifted)
    ).astype(jnp.bfloat16)


def on_device(
    flux_field,
    footprint,
    block_index,
    tile_count,
    sounding_week,
    member_ids,
    observed,
    perturb,
    obs_weight,
):
    slab_rows = lax.all_gather(flux_field, "obs", axis=1, tiled=True)[0]
    slab_count = slab_rows.shape[0]
    slots = footprint.shape[0]
    sounds = footprint.shape[2]
    cells = footprint.shape[3]
    rows_all = WEEKS * MEMBERS
    chosen = slab_rows[block_index]
    mixing = jnp.einsum("tkrc,tksc->trs", chosen, footprint, preferred_element_type=jnp.float32)
    mixing = mixing.reshape(slots, WEEKS, MEMBERS, sounds)
    week_ids = jnp.arange(WEEKS, dtype=jnp.int32)
    week_hot = (sounding_week[:, None, :] == week_ids[None, :, None]).astype(jnp.float32)
    partial_value = jnp.einsum("twms,tws->tms", mixing, week_hot, precision=lax.Precision.HIGHEST)
    alive = (jnp.arange(slots, dtype=jnp.int32) < tile_count[0]).astype(jnp.float32)
    member_hot = (member_ids[:, None] == jnp.arange(MEMBERS, dtype=jnp.int32)[None, :]).astype(
        jnp.float32
    )
    shifted = jnp.einsum(
        "mk,tks->tms", member_hot, perturb.astype(jnp.float32), precision=lax.Precision.HIGHEST
    )
    modeled = lax.psum(partial_value, "cell")
    residual = weigh_misfit(modeled, alive, obs_weight, observed, shifted)
    week_mask = week_hot.astype(jnp.bfloat16)
    flat_blocks = block_index.reshape(-1)
    adjoint_rows = (residual[:, None, :, :] * week_mask[:, :, None, :]).reshape(
        slots, rows_all, sounds
    )
    contrib = jnp.einsum(
        "trs,tksc->tkrc", adjoint_rows, footprint, preferred_element_type=jnp.float32
    )
    partial_grad = jax.ops.segment_sum(
        contrib.reshape(-1, rows_all, cells), flat_blocks, num_segments=slab_count
    )
    gradient = lax.psum_scatter(partial_grad, "obs", scatter_dimension=0, tiled=True)
    return (gradient[None], residual)


def solution(mesh):
    return jax.shard_map(
        on_device,
        mesh=mesh,
        in_specs=(
            P("cell", "obs", None, None),
            P("obs", "cell", None, None),
            P("obs", "cell"),
            P("obs"),
            P("obs", None),
            P(),
            P("obs", None),
            P("obs", None, None),
            P("obs", None),
        ),
        out_specs=(P("cell", "obs", None, None), P("obs", None, None)),
        check_vma=False,
    )
```

profile of v0, /device:TPU:0, one launch (start us, length us, event | category | flops | bytes accessed | tf_op | source)
XLA Modules:
  0.0 140.3 jit_solution(12556074545440462448)
XLA Ops:
  7.2 0.0 copy-start
  7.2 0.0 all-reduce.2.cloned.1.call-start
  7.2 0.7 compare_select_fusion
  7.9 0.1 copy.17
  8.0 0.1 reshape.36
  8.1 0.7 fusion.4
  8.8 24.0 %all_gather.3 = bf16[1,16,64,128]{3,2,0,1:T(8,128)(2,1)S(1)} all-gather(bf16[1,1,64,128]{3,2,0,1:T(8,128)(2,1)} %bitcast.47), channel_id=1, replica_groups=mesh['obs'=16,'cell'=2] {'obs'}, dimensions={1}, use_global_device_ids=true | all-gather | bytes 278528 | tf_op jit(solution)/shard_map/all_gather | solution.py:27
  32.8 0.9 gather_fusion
  33.8 0.0 copy-start.3
  33.8 0.0 copy-start.5
  33.8 0.0 copy-start.4
  33.8 0.0 copy-start.6
  33.8 3.7 %fusion.8 = f32[16,64,128,1]{2,1,3,0:T(8,128)S(1)} fusion(bf16[16,8,64,128]{3,2,1,0:T(8,128)(2,1)S(1)} %bitcast.43, bf16[16,8,128,128]{3,2,1,0:T(8,128)(2,1)} %param.10), kind=kOutput, calls=%fused_computation.19 | convolution fusion | flops 268435456 | bytes 6815744 | tf_op jit(solution)/shard_map/tkrc,tksc->trs/dot_general | solution.py:34
  37.6 0.7 multiply_reduce_fusion
  38.3 0.0 all-reduce.2.cloned.1.call-update
  38.3 0.0 reduce-scatter.2.cloned.1.call-start
  38.3 0.0 copy-done.3
  38.4 0.1 copy.15
  39.1 0.1 reshape.44
  39.2 0.0 copy-done.5
  39.2 0.1 broadcast_multiply_fusion.1
  39.3 17.9 %all-reduce.2.cloned.1.call-done = f32[16,16,128]{2,1,0:T(8,128)} async-done(((f32[16,16,128]{2,1,0:T(8,128)}), f32[16,16,128]{2,1,0:T(8,128)}) %all-reduce.2.cloned.1.call-update) | async-done | bytes 131088 | tf_op jit(solution)/shard_map/psum | solution.py:46
  57.2 0.0 copy-done
  57.2 0.0 copy-done.4
  57.2 0.0 copy-done.6
  57.2 1.1 fusion.2
  58.3 0.0 copy-start.2
  58.4 4.8 %fusion.9 = f32[16,64,8,128]{3,1,2,0:T(8,128)} fusion(bf16[16,64,128,1]{2,1,3,0:T(8,128)(2,1)S(1)} %bitcast.45, bf16[16,8,128,128]{3,2,1,0:T(8,128)(2,1)} %param.10), kind=kOutput, calls=%fused_computation.20 | convolution fusion | flops 268435456 | bytes 8650752 | tf_op jit(solution)/shard_map/trs,tksc->tkrc/dot_general | solution.py:53
  63.3 13.5 %scatter_fusion = f32[16,64,128]{2,1,0:T(8,128)S(1)} fusion(f32[16,64,128]{2,1,0:T(8,128)S(1)} %broadcast_in_dim.6, s32[128]{0:T(128)S(1)} %reshape.44, f32[128,64,128]{2,1,0:T(8,128)} %bitcast.42), kind=kCustom, calls=%fused_computation.1 | custom fusion | flops 1048576 | bytes 12583424 | tf_op jit(solution)/shard_map/scatter-add | solution.py:56
  76.8 0.8 copy-done.1
  77.6 0.0 reduce-scatter.2.cloned.1.call-update
  77.6 55.9 %reduce-scatter.2.cloned.1.call-done = f32[1,64,128]{2,1,0:T(8,128)} async-done(((f32[16,64,128]{2,1,0:T(8,128)}), f32[1,64,128]{2,1,0:T(8,128)}) %reduce-scatter.2.cloned.1.call-update) | async-done | bytes 32784 | tf_op jit(solution)/shard_map/reduce_scatter | solution.py:59
  (6 shorter events, 0.1 us)
Async XLA Ops:
  7.2 50.0 %copy-start = (bf16[16,16,128]{2,1,0:T(8,128)(2,1)S(1)}, bf16[16,16,128]{2,1,0:T(8,128)(2,1)}, u32[]{:S(2)}) copy-start(bf16[16,16,128]{2,1,0:T(8,128)(2,1)} %param.16) | copy-start | bytes 196612
  7.2 50.0 %all-reduce.2.cloned.1.call-start = ((), (), s32[]{:S(2)}) async-start(), calls=%async_computation.1 | async-start | bytes 262144 | tf_op jit(solution)/shard_map/psum | solution.py:46
  33.8 4.6 %copy-start.3 = (s32[16,8]{0,1:T(8,128)S(1)}, s32[16,8]{0,1:T(8,128)}, u32[]{:S(2)}) copy-start(s32[16,8]{0,1:T(8,128)} %param.11) | copy-start | bytes 1540
  33.8 5.4 %copy-start.5 = (f32[16,128]{1,0:T(8,128)S(1)}, f32[16,128]{1,0:T(8,128)}, u32[]{:S(2)}) copy-start(f32[16,128]{1,0:T(8,128)} %param.17) | copy-start | bytes 24580
  33.8 23.4 %copy-start.4 = (f32[16,128]{1,0:T(8,128)S(1)}, f32[16,128]{1,0:T(8,128)}, u32[]{:S(2)}) copy-start(f32[16,128]{1,0:T(8,128)} %param.15) | copy-start | bytes 24580
  33.8 23.4 %copy-start.6 = (s32[16]{0:T(128)S(1)}, s32[16]{0:T(128)}, u32[]{:S(2)}) copy-start(s32[16]{0:T(128)} %param.14) | copy-start | bytes 196
  38.3 95.2 %reduce-scatter.2.cloned.1.call-start = ((), (), s32[]{:S(2)}) async-start(), calls=%async_computation.2 | async-start | bytes 557056 | tf_op jit(solution)/shard_map/reduce_scatter | solution.py:59
  58.3 4.9 %copy-start.2 = (bf16[16,16,128]{2,1,0:T(8,128)(2,1)}, bf16[16,16,128]{2,1,0:T(8,128)(2,1)S(1)}, u32[]{:S(2)}) copy-start(bf16[16,16,128]{2,1,0:T(8,128)(2,1)S(1)} %fusion.2) | copy-start | bytes 196612
  76.8 0.8 copy-start.1
Sparse Core Ops, SparseCore 0:
  38.4 18.7 all-reduce.1
  77.7 55.7 reduce-scatter.1
where the time goes:
time: 141 us; the launch traced here: 140 us
  waiting for transfers between devices  73.8 us (52%)
  blocking collectives  24 us (17%)
  other arithmetic  15.7 us (11%)
  between operations  14.8 us (10%)
  matrix products  9.68 us (7%)
  local copies, waits for them, and re-layouts  2.14 us (2%)
    reduce_scatter x1, waiting for transfers between devices, on_device(): lax.psum_scatter(partial_grad, 'obs', scatter_dimension=0, tiled=True)  55.9 us
    all_gather x1, blocking collectives, on_device(): slab_rows = lax.all_gather(flux_field, 'obs', axis=1, tiled=True)[0]  24 us
    psum x1, waiting for transfers between devices, on_device(): modeled = lax.psum(partial_value, 'cell')  17.9 us
    scatter-add x1, other arithmetic, on_device(): jax.ops.segment_sum(contrib.reshape(-1, rows_all, cells), flat_blocks, nu...  13.5 us
    dot_general x1, matrix products, on_device(): jnp.einsum('trs,tksc->tkrc', adjoint_rows, footprint, preferred_element_t...  4.84 us
    dot_general x1, matrix products, on_device(): jnp.einsum('tkrc,tksc->trs', chosen, footprint, preferred_element_type=jn...  3.73 us
  transfers between devices with their start and end apart: 2, of which 2 were waited for; matrix products, arithmetic and copies ran while one was open for 0% of the time, Pallas kernels for 0%

commit v1 on v0

--- a/solution.py
+++ b/solution.py
@@ -43,7 +43,7 @@
     shifted = jnp.einsum(
         "mk,tks->tms", member_hot, perturb.astype(jnp.float32), precision=lax.Precision.HIGHEST
     )
-    modeled = lax.psum(partial_value, "cell")
+    modeled = jnp.sum(lax.all_gather(partial_value, "cell"), axis=0)
     residual = weigh_misfit(modeled, alive, obs_weight, observed, shifted)
     week_mask = week_hot.astype(jnp.bfloat16)
     flat_blocks = block_index.reshape(-1)

time: 141 us -> 126 us (0.89)
  waiting for transfers between devices: 73.8 us -> 53.2 us
  blocking collectives: 24 us -> 30.5 us
    psum x1 -> x0, waiting for transfers between devices: 17.9 us -> none  [on_device(): modeled = lax.psum(partial_value, 'cell')]
    all_gather x0 -> x1, blocking collectives: none -> 6.43 us  [on_device(): modeled = jnp.sum(lax.all_gather(partial_value, 'cell'), axis=0)]
    reduce_scatter x1, waiting for transfers between devices: 55.9 us -> 53.2 us  [on_device(): lax.psum_scatter(partial_grad, 'obs', scatter_dimension=0, tiled=True)]
  transfers between devices with their start and end apart: 2 -> 1, of which waited for: 2 -> 1; matrix products, arithmetic and copies ran while one was open for 0% -> 0% of each run, Pallas kernels for 0% -> 0%
where the time goes in v1:
time: 126 us; the launch traced here: 125 us
  waiting for transfers between devices  53.2 us (42%)
  blocking collectives  30.5 us (24%)
  other arithmetic  15.1 us (12%)
  between operations  14.8 us (12%)
  matrix products  8.76 us (7%)
  local copies, waits for them, and re-layouts  2.81 us (2%)
    reduce_scatter x1, waiting for transfers between devices, on_device(): lax.psum_scatter(partial_grad, 'obs', scatter_dimension=0, tiled=True)  53.2 us
    all_gather x1, blocking collectives, on_device(): slab_rows = lax.all_gather(flux_field, 'obs', axis=1, tiled=True)[0]  24 us
    scatter-add x1, other arithmetic, on_device(): jax.ops.segment_sum(contrib.reshape(-1, rows_all, cells), flat_blocks, nu...  13.5 us
    all_gather x1, blocking collectives, on_device(): modeled = jnp.sum(lax.all_gather(partial_value, 'cell'), axis=0)  6.43 us
    dot_general x1, matrix products, on_device(): jnp.einsum('trs,tksc->tkrc', adjoint_rows, footprint, preferred_element_t...  4.82 us
    dot_general x1, matrix products, on_device(): jnp.einsum('tkrc,tksc->trs', chosen, footprint, preferred_element_type=jn...  3.72 us
  transfers between devices with their start and end apart: 1, of which 1 were waited for; matrix products, arithmetic and copies ran while one was open for 0% of the time, Pallas kernels for 0%

profile of v1, /device:TPU:0, one launch (start us, length us, event | category | flops | bytes accessed | tf_op | source)
XLA Modules:
  0.0 125.2 jit_solution(9855843519054582420)
XLA Ops:
  7.2 0.0 copy-start
  7.2 0.0 reduce-scatter.2.cloned.1.call-start
  7.2 0.7 compare_select_fusion
  7.9 0.8 copy.15
  9.3 0.1 copy.17
  9.4 0.1 reshape.36
  9.5 0.1 reshape.44
  9.6 0.7 fusion.4
  10.3 24.0 %all_gather.9 = bf16[1,16,64,128]{3,2,0,1:T(8,128)(2,1)S(1)} all-gather(bf16[1,1,64,128]{3,2,0,1:T(8,128)(2,1)} %bitcast.49), channel_id=1, replica_groups=mesh['obs'=16,'cell'=2] {'obs'}, dimensions={1}, use_global_device_ids=true | all-gather | bytes 278528 | tf_op jit(solution)/shard_map/all_gather | solution.py:27
  34.3 0.9 gather_fusion
  35.3 0.0 copy-start.4
  35.3 0.0 copy-start.3
  35.3 0.0 copy-start.5
  35.3 3.7 %fusion.8 = f32[16,64,128,1]{2,1,3,0:T(8,128)S(1)} fusion(bf16[16,8,64,128]{3,2,1,0:T(8,128)(2,1)S(1)} %bitcast.44, bf16[16,8,128,128]{3,2,1,0:T(8,128)(2,1)} %param.10), kind=kOutput, calls=%fused_computation.19 | convolution fusion | flops 268435456 | bytes 6815744 | tf_op jit(solution)/shard_map/tkrc,tksc->trs/dot_general | solution.py:34
  39.1 0.1 multiply_reduce_fusion
  39.1 6.4 %all-gather = f32[32,16,128]{2,1,0:T(8,128)S(1)} all-gather(f32[16,16,128]{2,1,0:T(8,128)S(1)} %bitcast.48), channel_id=2, replica_groups=mesh['obs'=16,'cell'=2] {'cell'}, dimensions={0}, use_global_device_ids=true | all-gather | bytes 393216 | tf_op jit(solution)/shard_map/all_gather | solution.py:46
  45.6 0.0 copy-done.4
  45.6 0.1 broadcast_multiply_fusion.1
  45.6 0.0 copy-done
  45.7 0.0 copy-done.3
  45.7 0.0 copy-done.5
  45.7 0.2 fusion.2
  45.9 0.0 copy-start.2
  45.9 4.8 %fusion.9 = f32[16,64,8,128]{3,1,2,0:T(8,128)} fusion(bf16[16,64,128,1]{2,1,3,0:T(8,128)(2,1)S(1)} %bitcast.46, bf16[16,8,128,128]{3,2,1,0:T(8,128)(2,1)} %param.10), kind=kOutput, calls=%fused_computation.20 | convolution fusion | flops 268435456 | bytes 8650752 | tf_op jit(solution)/shard_map/trs,tksc->tkrc/dot_general | solution.py:53
  50.8 0.0 copy-done.2
  50.8 13.5 %scatter_fusion = f32[16,64,128]{2,1,0:T(8,128)S(1)} fusion(f32[16,64,128]{2,1,0:T(8,128)S(1)} %broadcast_in_dim.6, s32[128]{0:T(128)S(1)} %reshape.44, f32[128,64,128]{2,1,0:T(8,128)} %bitcast.43), kind=kCustom, calls=%fused_computation.1 | custom fusion | flops 1048576 | bytes 12583424 | tf_op jit(solution)/shard_map/scatter-add | solution.py:56
  64.3 0.0 copy-start.1
  64.4 0.8 copy-done.1
  65.1 0.0 reduce-scatter.2.cloned.1.call-update
  65.2 53.2 %reduce-scatter.2.cloned.1.call-done = f32[1,64,128]{2,1,0:T(8,128)} async-done(((f32[16,64,128]{2,1,0:T(8,128)}), f32[1,64,128]{2,1,0:T(8,128)}) %reduce-scatter.2.cloned.1.call-update) | async-done | bytes 32784 | tf_op jit(solution)/shard_map/reduce_scatter | solution.py:59
  (5 shorter events, 0.1 us)
Async XLA Ops:
  7.2 38.5 %copy-start = (bf16[16,16,128]{2,1,0:T(8,128)(2,1)S(1)}, bf16[16,16,128]{2,1,0:T(8,128)(2,1)}, u32[]{:S(2)}) copy-start(bf16[16,16,128]{2,1,0:T(8,128)(2,1)} %param.16) | copy-start | bytes 196612
  7.2 111.2 %reduce-scatter.2.cloned.1.call-start = ((), (), s32[]{:S(2)}) async-start(), calls=%async_computation.1 | async-start | bytes 557056 | tf_op jit(solution)/shard_map/reduce_scatter | solution.py:59
  35.3 10.3 %copy-start.4 = (f32[16,128]{1,0:T(8,128)S(1)}, f32[16,128]{1,0:T(8,128)}, u32[]{:S(2)}) copy-start(f32[16,128]{1,0:T(8,128)} %param.17) | copy-start | bytes 24580
  35.3 10.4 %copy-start.3 = (f32[16,128]{1,0:T(8,128)S(1)}, f32[16,128]{1,0:T(8,128)}, u32[]{:S(2)}) copy-start(f32[16,128]{1,0:T(8,128)} %param.15) | copy-start | bytes 24580
  35.3 10.3 %copy-start.5 = (s32[16]{0:T(128)S(1)}, s32[16]{0:T(128)}, u32[]{:S(2)}) copy-start(s32[16]{0:T(128)} %param.14) | copy-start | bytes 196
  45.9 4.9 %copy-start.2 = (bf16[16,16,128]{2,1,0:T(8,128)(2,1)}, bf16[16,16,128]{2,1,0:T(8,128)(2,1)S(1)}, u32[]{:S(2)}) copy-start(bf16[16,16,128]{2,1,0:T(8,128)(2,1)S(1)} %fusion.2) | copy-start | bytes 196612
  64.3 0.8 copy-start.1
Sparse Core Ops, SparseCore 0:
  65.3 53.0 reduce-scatter.1
